TPU v7x, 32 devices: a whole 2x2x4 slice. The times are simulated.
32 devices in a mesh: ctx: 8 (over z, core), head: 4 (over y, x).
Axes of the slice: x: 2, y: 2, z: 4, core: 2. Of those that a mesh axis runs over, the one named last changes fastest.
Arguments:
- queries: bfloat16 [1024, 8192], P('ctx', 'head'), parts along dimension 1, may hold values from -17 to 17
- keys: bfloat16 [1024, 512], P('ctx', 'head'), parts along dimension 1, may hold values from -17 to 17
- values: bfloat16 [1024, 512], P('ctx', 'head'), parts along dimension 1, may hold values from -6 to 6
- block_position: int32 [8], P('ctx'), may hold values from 0 to 7, each once
Outputs:
- attended: bfloat16 [1024, 8192], P('ctx', 'head'), parts along dimension 1
There are 4 independent parts, one for each index of `head`. A program takes and returns all parts, laid end to end along the dimension named above; an argument that names none is the same for every part. Nothing has to cross between parts.
All inputs are finite; a program needn't handle non-finite values.
Results may differ from a plain program's by a relative error of at most 0.005.
Values may be sent and summed in bfloat16 or wider, within the bound.
No kernel may reach another device: no remote copies, remote signals or barrier semaphores. Data moves between devices by JAX's collectives and lax.ppermute only.
A program may use at most 128 MiB of HBM per device.

v0:
```python
import math
import jax
import jax.numpy as jnp
from jax import lax
from jax.sharding import PartitionSpec as P

HEAD_DIM = 128
QHEADS = 16
BLOCK = 128


def body(queries, keys, values, block_position):
    local_rows = queries.shape[0]
    places = lax.all_gather(block_position, "ctx", axis=0, tiled=True)
    myself = lax.axis_index("ctx")
    row_ids = myself * local_rows + jnp.arange(local_rows, dtype=jnp.int32)
    query_pos = jnp.take(places, row_ids // BLOCK) * BLOCK + row_ids % BLOCK
    latest = jnp.max(query_pos)
    query_heads = queries.reshape(local_rows, QHEADS, HEAD_DIM).transpose(1, 0, 2)
    scale = 1.0 / math.sqrt(HEAD_DIM)
    initial = (
        jnp.full((QHEADS, local_rows), -1e30, jnp.float32),
        jnp.zeros((QHEADS, local_rows), jnp.float32),
        jnp.zeros((QHEADS, local_rows, HEAD_DIM), jnp.float32),
    )
    key_piece = lax.all_gather(keys, "ctx", axis=0, tiled=True)
    value_piece = lax.all_gather(values, "ctx", axis=0, tiled=True)
    piece_rows = key_piece.shape[0]
    key_ids = jnp.arange(piece_rows, dtype=jnp.int32)
    key_pos = jnp.take(places, key_ids // BLOCK) * BLOCK + key_ids % BLOCK

    def attend(state_in):
        running_max, denominator, numerator = state_in
        scores = (
            jnp.einsum("htd,nd->htn", query_heads, key_piece, preferred_element_type=jnp.float32)
            * scale
        )
        visible = key_pos[None, None, :] <= query_pos[None, :, None]
        new_max = jnp.maximum(running_max, jnp.max(jnp.where(visible, scores, -1e30), axis=-1))
        weights = jnp.where(visible, jnp.exp(scores - new_max[..., None]), 0.0)
        denominator = jnp.sum(weights, axis=-1)
        numerator = jnp.einsum(
            "htn,nd->htd",
            weights.astype(jnp.bfloat16),
            value_piece,
            preferred_element_type=jnp.float32,
        )
        return (new_max, denominator, numerator)

    final = lax.cond(jnp.min(key_pos) > latest, lambda state_in: state_in, attend, initial)
    running_max, denominator, numerator = final
    output = (numerator / denominator[..., None]).astype(jnp.bfloat16)
    return output.transpose(1, 0, 2).reshape(local_rows, QHEADS * HEAD_DIM)


def solution(mesh):
    placed = (P("ctx", "head"), P("ctx", "head"), P("ctx", "head"), P("ctx"))
    return jax.shard_map(
        body, mesh=mesh, in_specs=placed, out_specs=P("ctx", "head"), check_vma=False
    )
```

profile of v0, /device:TPU:0, one launch (start us, length us, event | category | flops | bytes accessed | tf_op | source)
XLA Modules:
  0.0 63.8 jit_solution(7075929578409433718)
XLA Ops:
  0.7 1.2 %dynamic-slice = u32[1]{0:T(128)} dynamic-slice(u32[32]{0:T(128)} %constant.118, u32[]{:T(128)S(6)} %add.115), dynamic_slice_sizes={1} | dynamic-slice | bytes 12
  1.9 0.8 %dynamic-update-slice = s32[8]{0:T(128)S(1)} dynamic-update-slice(s32[8]{0:T(128)S(1)} %broadcast.303, s32[1]{0:T(128)S(6)} %copy.17, u32[]{:T(128)} %bitcast.2) | dynamic-update-slice | bytes 12
  2.7 10.6 %all-reduce = s32[8]{0:T(128)S(1)} all-reduce(s32[8]{0:T(128)S(1)} %dynamic-update-slice), channel_id=1, replica_groups=mesh['ctx'=8,'head'=4] {'ctx'}, use_global_device_ids=true, to_apply=%add | all-reduce | flops 8 | bytes 64
  13.3 0.7 %fusion.29 = (s32[1]{0:T(128)}, s32[1]{0:T(128)}, s32[1]{0:T(128)}, s32[1]{0:T(128)}, s32[1]{0:T(128)}, /*index=5*/s32[1]{0:T(128)}, s32[1]{0:T(128)}, s32[1]{0:T(128)}) fusion(s32[8]{0:T(128)S(1)} %all-reduce), kind=kLoop, calls=%fused_computation.69 | loop fusion | bytes 64 | tf_op jit(solution)/shard_map/jit(_take)/gather | solution.py:30
  14.0 5.7 %fusion.25 = (s32[]{:T(128)}, s32[128]{0:T(128)S(1)}) fusion(s32[]{:T(128)} %bitcast.10, s32[]{:T(128)} %bitcast.9, s32[]{:T(128)} %bitcast.8, s32[]{:T(128)} %bitcast.7, s32[]{:T(128)} %bitcast.6, s32[]{:T(128)} %bitcast.5, s32[]{:T(128)} %bitcast.4, s32[]{:T(128)} %bitcast.3, s32[]{:T(128)S(6)} %mul.15), kind=kLoop, calls=%fused_computation.67 | loop fusion | flops 8063 | bytes 552 | tf_op jit(solution)/shard_map/reduce_max | solution.py:18
  19.7 4.3 %compare_select_fusion.1 = s32[1024,1]{0,1:T(1,128)S(1)} fusion(s32[]{:T(128)} %bitcast.4, s32[]{:T(128)} %bitcast.5, s32[]{:T(128)} %bitcast.6, s32[]{:T(128)} %bitcast.7, s32[]{:T(128)} %bitcast.8, s32[]{:T(128)} %bitcast.10, s32[]{:T(128)} %bitcast.9), kind=kLoop, calls=%fused_computation.18 | loop fusion | flops 23552 | bytes 4124 | tf_op jit(solution)/shard_map/jit(_take)/gather | solution.py:30
  24.0 1.3 %fusion.27 = (s32[]{:T(128)}, s32[1024]{0:T(1024)S(1)}) fusion(pred[1024]{0:T(1024)(128)(4,1)S(1)} %compare_reduce_fusion, s32[1024]{0:T(1024)S(1)} %bitcast.45, s32[]{:T(128)} %bitcast.3), kind=kLoop, calls=%fused_computation.68 | loop fusion | flops 23551 | bytes 9224 | tf_op jit(solution)/shard_map/reduce_min | solution.py:50
  26.5 14.4 %all_gather.10 = bf16[1024,128]{1,0:T(8,128)(2,1)S(1)} all-gather(bf16[128,128]{1,0:T(8,128)(2,1)} %param.7), channel_id=1, replica_groups=mesh['ctx'=8,'head'=4] {'ctx'}, dimensions={0}, use_global_device_ids=true | all-gather | bytes 294912 | tf_op jit(solution)/shard_map/all_gather | solution.py:26
  40.9 14.4 %all_gather.11 = bf16[1024,128]{1,0:T(8,128)(2,1)S(1)} all-gather(bf16[128,128]{1,0:T(8,128)(2,1)} %param.8), channel_id=1, replica_groups=mesh['ctx'=8,'head'=4] {'ctx'}, dimensions={0}, use_global_device_ids=true | all-gather | bytes 294912 | tf_op jit(solution)/shard_map/all_gather | solution.py:27
  55.3 1.3 %copy.6 = bf16[128,2048]{0,1:T(8,128)(2,1)S(1)} copy(bf16[128,2048]{1,0:T(8,128)(2,1)} %param.6) | data formatting | bytes 1048576 | tf_op args[0]
  56.6 6.0 %conditional.1 = (f32[16,128]{1,0:T(8,128)S(1)}, f32[16,128,128]{2,1,0:T(8,128)S(1)}) conditional(s32[]{:T(128)} %convert_element_type.9, (s32[1024]{0:T(1024)S(1)}, s32[128]{0:T(128)S(1)}, bf16[16,128,128]{1,2,0:T(8,128)(2,1)S(1)}, bf16[1024,128]{1,0:T(8,128)(2,1)S(1)}, bf16[1024,128]{1,0:T(8,128)(2,1)S(1)}) %tuple.28, () %tuple.14), branch_computations={%region_2.5_spmd, %region_5.6_spmd} | conditional | flops 1096939520 | bytes 27841040 | solution.py:50
  56.6 0.1 broadcast_compare_fusion
  56.8 1.6 %select_reduce_fusion = (f32[16,128]{1,0:T(8,128)S(1)}, f32[16,128,1024]{2,1,0:T(8,128)S(1)}) fusion(pred[128,1024]{1,0:T(8,128)(4,1)S(1)} %broadcast_compare_fusion, bf16[16,128,128]{1,2,0:T(8,128)(2,1)S(1)} %get-tuple-element.26, bf16[1024,128]{1,0:T(8,128)(2,1)S(1)} %get-tuple-element.18), kind=kOutput, calls=%fused_computation.1 | convolution fusion | flops 543160320 | bytes 9314304 | tf_op jit(solution)/shard_map/cond/branch_0_fun/htd,nd->htn/dot_general | solution.py:35
  58.4 2.4 %fusion.1 = f32[16,128]{1,0:T(8,128)S(1)} fusion(f32[16,128,1024]{2,1,0:T(8,128)S(1)} %get-tuple-element.34, f32[16,128]{1,0:T(8,128)S(1)} %broadcast_maximum_fusion, pred[128,1024]{1,0:T(8,128)(4,1)S(1)} %broadcast_compare_fusion), kind=kLoop, calls=%fused_computation.3 | loop fusion | flops 8386560 | bytes 8536064 | tf_op jit(solution)/shard_map/cond/branch_0_fun/reduce_sum | solution.py:41
  60.8 1.8 %fusion.2 = f32[16,128,128]{2,1,0:T(8,128)S(1)} fusion(f32[16,128,1024]{2,1,0:T(8,128)S(1)} %get-tuple-element.34, f32[16,128]{1,0:T(8,128)S(1)} %broadcast_maximum_fusion, pred[128,1024]{1,0:T(8,128)(4,1)S(1)} %broadcast_compare_fusion, bf16[1024,128]{1,0:T(8,128)(2,1)S(1)} %get-tuple-element.19), kind=kOutput, calls=%fused_computation.4 | convolution fusion | flops 545259520 | bytes 9838592 | tf_op jit(solution)/shard_map/cond/branch_0_fun/htn,nd->htd/dot_general | solution.py:42
  62.7 1.1 %copy_bitcast_fusion = bf16[128,2048]{1,0:T(8,128)(2,1)} fusion(f32[16,128,128]{2,1,0:T(8,128)S(1)} %get-tuple-element.22, f32[16,128]{1,0:T(8,128)S(1)} %get-tuple-element.23), kind=kLoop, calls=%fused_computation.14 | loop fusion | flops 524288 | bytes 1581056 | tf_op jit(solution)/shard_map/reshape | solution.py:53
  (3 shorter events, 0.0 us)
where the time goes:
time: 64.2 us; the launch traced here: 63.8 us
  blocking collectives  39.4 us (61%)
  other arithmetic  15 us (23%)
  local copies, waits for them, and re-layouts  4 us (6%)
  matrix products  3.44 us (5%)
  between operations  1.94 us (3%)
    all_gather x1, blocking collectives, body(): key_piece = lax.all_gather(keys, 'ctx', axis=0, tiled=True)  14.4 us
    all_gather x1, blocking collectives, body(): value_piece = lax.all_gather(values, 'ctx', axis=0, tiled=True)  14.4 us
    unnamed x1, blocking collectives  10.6 us
    reduce_max x1, other arithmetic, body(): latest = jnp.max(query_pos)  5.67 us
    gather x2, other arithmetic, body(): key_pos = jnp.take(places, key_ids // BLOCK) * BLOCK + key_ids % BLOCK  4.32 us
    unnamed x4, local copies, waits for them, and re-layouts  3.31 us
    reduce_sum x1, other arithmetic, attend(): denominator = jnp.sum(weights, axis=-1)  2.41 us
    dot_general x1, matrix products, attend(): jnp.einsum('htn,nd->htd', weights.astype(jnp.bfloat16), value_piece, pref...  1.84 us

commit v1 on v0

--- a/solution.py
+++ b/solution.py
@@ -23,8 +23,11 @@
         jnp.zeros((QHEADS, local_rows), jnp.float32),
         jnp.zeros((QHEADS, local_rows, HEAD_DIM), jnp.float32),
     )
-    key_piece = lax.all_gather(keys, "ctx", axis=0, tiled=True)
-    value_piece = lax.all_gather(values, "ctx", axis=0, tiled=True)
+    key_piece, value_piece = jnp.split(
+        lax.all_gather(jnp.concatenate([keys, values], axis=1), "ctx", axis=0, tiled=True),
+        [keys.shape[1]],
+        axis=1,
+    )
     piece_rows = key_piece.shape[0]
     key_ids = jnp.arange(piece_rows, dtype=jnp.int32)
     key_pos = jnp.take(places, key_ids // BLOCK) * BLOCK + key_ids % BLOCK

time: 64.2 us -> 51 us (0.79)
  blocking collectives: 39.4 us -> 25.5 us
  other arithmetic: 15 us -> 15.7 us
    all_gather x2 -> x1, blocking collectives: 28.8 us -> 14.8 us  [body(): lax.all_gather(jnp.concatenate([keys, values], axis=1), 'ctx', axis=0, ti...]
    concatenate x0 -> x1, other arithmetic: none -> 0.79 us  [body(): jnp.concatenate([keys, values], axis=1)]
where the time goes in v1:
time: 51 us; the launch traced here: 50.6 us
  blocking collectives  25.5 us (50%)
  other arithmetic  15.7 us (31%)
  local copies, waits for them, and re-layouts  4 us (8%)
  matrix products  3.36 us (7%)
  between operations  1.94 us (4%)
    all_gather x1, blocking collectives, body(): lax.all_gather(jnp.concatenate([keys, values], axis=1), 'ctx', axis=0, ti...  14.8 us
    unnamed x1, blocking collectives  10.6 us
    reduce_max x1, other arithmetic, body(): latest = jnp.max(query_pos)  5.67 us
    gather x2, other arithmetic, body(): key_pos = jnp.take(places, key_ids // BLOCK) * BLOCK + key_ids % BLOCK  4.32 us
    unnamed x4, local copies, waits for them, and re-layouts  3.31 us
    reduce_sum x1, other arithmetic, attend(): denominator = jnp.sum(weights, axis=-1)  2.41 us
    dot_general x1, matrix products, attend(): jnp.einsum('htn,nd->htd', weights.astype(jnp.bfloat16), value_piece, pref...  1.76 us
    dot_general x1, matrix products, attend(): jnp.einsum('htd,nd->htn', query_heads, key_piece, preferred_element_type=...  1.61 us

profile of v1, /device:TPU:0, one launch (start us, length us, event | category | flops | bytes accessed | tf_op | source)
XLA Modules:
  0.0 50.6 jit_solution(2110458882428455873)
XLA Ops:
  0.7 1.2 %dynamic-slice = u32[1]{0:T(128)} dynamic-slice(u32[32]{0:T(128)} %constant.118, u32[]{:T(128)S(6)} %add.115), dynamic_slice_sizes={1} | dynamic-slice | bytes 12
  1.9 0.8 %dynamic-update-slice = s32[8]{0:T(128)S(1)} dynamic-update-slice(s32[8]{0:T(128)S(1)} %broadcast.303, s32[1]{0:T(128)S(6)} %copy.17, u32[]{:T(128)} %bitcast.2) | dynamic-update-slice | bytes 12
  2.7 10.6 %all-reduce = s32[8]{0:T(128)S(1)} all-reduce(s32[8]{0:T(128)S(1)} %dynamic-update-slice), channel_id=1, replica_groups=mesh['ctx'=8,'head'=4] {'ctx'}, use_global_device_ids=true, to_apply=%add | all-reduce | flops 8 | bytes 64
  13.3 0.7 %fusion.31 = (s32[1]{0:T(128)}, s32[1]{0:T(128)}, s32[1]{0:T(128)}, s32[1]{0:T(128)}, s32[1]{0:T(128)}, /*index=5*/s32[1]{0:T(128)}, s32[1]{0:T(128)}, s32[1]{0:T(128)}) fusion(s32[8]{0:T(128)S(1)} %all-reduce), kind=kLoop, calls=%fused_computation.72 | loop fusion | bytes 64 | tf_op jit(solution)/shard_map/jit(_take)/gather | solution.py:33
  14.0 5.7 %fusion.27 = (s32[]{:T(128)}, s32[128]{0:T(128)S(1)}) fusion(s32[]{:T(128)} %bitcast.10, s32[]{:T(128)} %bitcast.9, s32[]{:T(128)} %bitcast.8, s32[]{:T(128)} %bitcast.7, s32[]{:T(128)} %bitcast.6, s32[]{:T(128)} %bitcast.5, s32[]{:T(128)} %bitcast.4, s32[]{:T(128)} %bitcast.3, s32[]{:T(128)S(6)} %mul.15), kind=kLoop, calls=%fused_computation.70 | loop fusion | flops 8063 | bytes 552 | tf_op jit(solution)/shard_map/reduce_max | solution.py:18
  19.7 4.3 %compare_select_fusion.1 = s32[1024,1]{0,1:T(1,128)S(1)} fusion(s32[]{:T(128)} %bitcast.4, s32[]{:T(128)} %bitcast.5, s32[]{:T(128)} %bitcast.6, s32[]{:T(128)} %bitcast.7, s32[]{:T(128)} %bitcast.8, s32[]{:T(128)} %bitcast.10, s32[]{:T(128)} %bitcast.9), kind=kLoop, calls=%fused_computation.21 | loop fusion | flops 23552 | bytes 4124 | tf_op jit(solution)/shard_map/jit(_take)/gather | solution.py:33
  24.0 1.3 %fusion.29 = (s32[]{:T(128)}, s32[1024]{0:T(1024)S(1)}) fusion(pred[1024]{0:T(1024)(128)(4,1)S(1)} %compare_reduce_fusion, s32[1024]{0:T(1024)S(1)} %bitcast.45, s32[]{:T(128)} %bitcast.3), kind=kLoop, calls=%fused_computation.71 | loop fusion | flops 23551 | bytes 9224 | tf_op jit(solution)/shard_map/reduce_min | solution.py:53
  26.5 0.8 %pad_maximum_fusion = bf16[128,256]{1,0:T(8,128)(2,1)S(1)} fusion(bf16[128,128]{1,0:T(8,128)(2,1)} %param.8, bf16[128,128]{1,0:T(8,128)(2,1)} %param.7), kind=kLoop, calls=%fused_computation.18 | loop fusion | flops 131072 | bytes 131072 | tf_op jit(solution)/shard_map/concatenate | solution.py:27
  27.3 14.8 %all_gather.7 = bf16[1024,256]{1,0:T(8,128)(2,1)S(1)} all-gather(bf16[128,256]{1,0:T(8,128)(2,1)S(1)} %pad_maximum_fusion), channel_id=1, replica_groups=mesh['ctx'=8,'head'=4] {'ctx'}, dimensions={0}, use_global_device_ids=true | all-gather | bytes 589824 | tf_op jit(solution)/shard_map/all_gather | solution.py:27
  42.1 1.3 %copy.6 = bf16[128,2048]{0,1:T(8,128)(2,1)S(1)} copy(bf16[128,2048]{1,0:T(8,128)(2,1)} %param.6) | data formatting | bytes 1048576 | tf_op args[0]
  43.5 6.0 %conditional.1 = (f32[16,128]{1,0:T(8,128)S(1)}, f32[16,128,128]{2,1,0:T(8,128)S(1)}) conditional(s32[]{:T(128)} %convert_element_type.9, (s32[1024]{0:T(1024)S(1)}, s32[128]{0:T(128)S(1)}, bf16[1024,256]{1,0:T(8,128)(2,1)S(1)}, bf16[16,128,128]{1,2,0:T(8,128)(2,1)S(1)}) %tuple.28, () %tuple.14), branch_computations={%region_2.5_spmd, %region_5.6_spmd} | conditional | flops 1096939520 | bytes 27841040 | solution.py:53
  43.5 0.1 broadcast_compare_fusion
  43.6 1.6 %select_reduce_fusion = (f32[16,128]{1,0:T(8,128)S(1)}, f32[16,128,1024]{2,1,0:T(8,128)S(1)}) fusion(pred[128,1024]{1,0:T(8,128)(4,1)S(1)} %broadcast_compare_fusion, bf16[16,128,128]{1,2,0:T(8,128)(2,1)S(1)} %get-tuple-element.27, bf16[1024,256]{1,0:T(8,128)(2,1)S(1)} %get-tuple-element.19), kind=kOutput, calls=%fused_computation.1 | convolution fusion | flops 543160320 | bytes 9314304 | tf_op jit(solution)/shard_map/cond/branch_0_fun/htd,nd->htn/dot_general | solution.py:38
  45.2 2.4 %fusion.1 = f32[16,128]{1,0:T(8,128)S(1)} fusion(f32[16,128,1024]{2,1,0:T(8,128)S(1)} %get-tuple-element.33, f32[16,128]{1,0:T(8,128)S(1)} %broadcast_maximum_fusion, pred[128,1024]{1,0:T(8,128)(4,1)S(1)} %broadcast_compare_fusion), kind=kLoop, calls=%fused_computation.3 | loop fusion | flops 8386560 | bytes 8536064 | tf_op jit(solution)/shard_map/cond/branch_0_fun/reduce_sum | solution.py:44
  47.7 1.8 %fusion.2 = f32[16,128,128]{2,1,0:T(8,128)S(1)} fusion(f32[16,128,1024]{2,1,0:T(8,128)S(1)} %get-tuple-element.33, f32[16,128]{1,0:T(8,128)S(1)} %broadcast_maximum_fusion, pred[128,1024]{1,0:T(8,128)(4,1)S(1)} %broadcast_compare_fusion, bf16[1024,256]{1,0:T(8,128)(2,1)S(1)} %get-tuple-element.19), kind=kOutput, calls=%fused_computation.4 | convolution fusion | flops 545259520 | bytes 9838592 | tf_op jit(solution)/shard_map/cond/branch_0_fun/htn,nd->htd/dot_general | solution.py:45
  49.4 1.1 %copy_bitcast_fusion = bf16[128,2048]{1,0:T(8,128)(2,1)} fusion(f32[16,128,128]{2,1,0:T(8,128)S(1)} %get-tuple-element.22, f32[16,128]{1,0:T(8,128)S(1)} %get-tuple-element.23), kind=kLoop, calls=%fused_computation.16 | loop fusion | flops 524288 | bytes 1581056 | tf_op jit(solution)/shard_map/reshape | solution.py:56
  (3 shorter events, 0.0 us)
